TPU v7x, 32 devices: a whole 2x2x4 slice. The times are simulated.
32 devices in a mesh: shard: 2 (over y), context: 4 (over z), tensor: 4 (over x, core).
Axes of the slice: x: 2, y: 2, z: 4, core: 2. Of those that a mesh axis runs over, the one named last changes fastest.
Arguments:
- inputs: bfloat16 [6, 2048, 768], P('shard', 'context'), may hold values from -6 to 6
- w_query: bfloat16 [768, 768], P('shard', 'tensor'), may hold values from -0.21875 to 0.21875
- b_query: float32 [768], P('tensor'), may hold values from -3 to 3
- w_key: bfloat16 [768, 768], P('shard', 'tensor'), may hold values from -0.21875 to 0.21875
- w_value: bfloat16 [768, 768], P('shard', 'tensor'), may hold values from -0.21875 to 0.21875
- b_value: float32 [768], P('tensor'), may hold values from -3 to 3
- w_out: bfloat16 [768, 768], P('tensor', 'shard'), may hold values from -3.5 to 3.5
- b_out: float32 [768], replicated, may hold values from -3 to 3
- first_gain: float32 [768], replicated, may hold values from 0.5 to 1.5
- first_bias: float32 [768], replicated, may hold values from -2 to 2
- w_hidden: bfloat16 [768, 3072], P('shard', 'tensor'), may hold values from -0.21875 to 0.21875
- b_hidden: float32 [3072], P('tensor'), may hold values from -3 to 3
- w_down: bfloat16 [3072, 768], P('tensor', 'shard'), may hold values from -0.109375 to 0.109375
- b_down: float32 [768], replicated, may hold values from -3 to 3
- second_gain: float32 [768], replicated, may hold values from 0.5 to 1.5
- second_bias: float32 [768], replicated, may hold values from -2 to 2
- cotangent: bfloat16 [6, 2048, 768], P('shard', 'context'), may hold values from -6 to 6
Outputs:
- outputs: bfloat16 [6, 2048, 768], P('shard', 'context')
- input_grad: bfloat16 [6, 2048, 768], P('shard', 'context')
- grad_w_query: float32 [768, 768], P('shard', 'tensor')
- grad_b_query: float32 [768], P('tensor')
- grad_w_key: float32 [768, 768], P('shard', 'tensor')
- grad_w_value: float32 [768, 768], P('shard', 'tensor')
- grad_b_value: float32 [768], P('tensor')
- grad_w_out: float32 [768, 768], P('tensor', 'shard')
- grad_b_out: float32 [768], replicated
- grad_first_gain: float32 [768], replicated
- grad_first_bias: float32 [768], replicated
- grad_w_hidden: float32 [768, 3072], P('shard', 'tensor')
- grad_b_hidden: float32 [3072], P('tensor')
- grad_w_down: float32 [3072, 768], P('tensor', 'shard')
- grad_b_down: float32 [768], replicated
- grad_second_gain: float32 [768], replicated
- grad_second_bias: float32 [768], replicated
All inputs are finite; a program needn't handle non-finite values.
Results may differ from a plain program's by a relative error of at most 0.018.
Values may be sent and summed in bfloat16 or wider, within the bound.
No kernel may reach another device: no remote copies, remote signals or barrier semaphores. Data moves between devices by JAX's collectives and lax.ppermute only.
A program may use at most 256 MiB of HBM per device.

v0:
```python
import jax
import jax.numpy as jnp
from jax import lax
from jax.sharding import PartitionSpec as P

HEAD_DIM = 64
MICRO = 3
EPSILON = 1e-05


def layer_norm(values, gain, bias):
    centre = jnp.mean(values, axis=-1, keepdims=True)
    centred = values - centre
    inverse = lax.rsqrt(jnp.mean(centred * centred, axis=-1, keepdims=True) + EPSILON)
    normed = centred * inverse
    return (normed * gain + bias, normed, inverse)


def norm_back(grad, normed, inverse, gain):
    scaled = grad * gain
    return inverse * (
        scaled
        - jnp.mean(scaled, axis=-1, keepdims=True)
        - normed * jnp.mean(scaled * normed, axis=-1, keepdims=True)
    )


def gelu_exact(values):
    return jax.nn.gelu(values, approximate=False)


def attend(queries, keys, values, factor):
    heads_here = queries.shape[-1] // HEAD_DIM
    results = []
    totals = []
    for head in range(heads_here):
        lower = head * HEAD_DIM
        upper = lower + HEAD_DIM
        scores = (
            jnp.einsum(
                "sqd,skd->sqk",
                queries[..., lower:upper],
                keys[..., lower:upper],
                preferred_element_type=jnp.float32,
            )
            * factor
        )
        log_total = jax.nn.logsumexp(scores, axis=-1, keepdims=True)
        low_probs = jnp.exp(scores - log_total).astype(jnp.bfloat16)
        results.append(
            jnp.einsum(
                "sqk,skd->sqd",
                low_probs,
                values[..., lower:upper],
                preferred_element_type=jnp.float32,
            )
        )
        totals.append(log_total)
    return (jnp.concatenate(results, axis=-1).astype(jnp.bfloat16), totals)


def attend_back(queries, keys, values, grad_heads, totals, factor):
    heads_here = queries.shape[-1] // HEAD_DIM
    grad_queries = []
    grad_keys = []
    grad_values = []
    for head in range(heads_here):
        lower = head * HEAD_DIM
        upper = lower + HEAD_DIM
        query_head = queries[..., lower:upper]
        key_head = keys[..., lower:upper]
        grad_head = grad_heads[..., lower:upper]
        scores = (
            jnp.einsum("sqd,skd->sqk", query_head, key_head, preferred_element_type=jnp.float32)
            * factor
        )
        attn_probs = jnp.exp(scores - totals[head])
        low_probs = attn_probs.astype(jnp.bfloat16)
        grad_probs = jnp.einsum(
            "sqd,skd->sqk", grad_head, values[..., lower:upper], preferred_element_type=jnp.float32
        )
        grad_values.append(
            jnp.einsum("sqk,sqd->skd", low_probs, grad_head, preferred_element_type=jnp.float32)
        )
        weighted = jnp.sum(attn_probs * grad_probs, axis=-1, keepdims=True)
        grad_scores = (attn_probs * (grad_probs - weighted)).astype(jnp.bfloat16)
        grad_queries.append(
            jnp.einsum("sqk,skd->sqd", grad_scores, key_head, preferred_element_type=jnp.float32)
            * factor
        )
        grad_keys.append(
            jnp.einsum("sqk,sqd->skd", grad_scores, query_head, preferred_element_type=jnp.float32)
            * factor
        )
    return (
        jnp.concatenate(grad_queries, axis=-1),
        jnp.concatenate(grad_keys, axis=-1),
        jnp.concatenate(grad_values, axis=-1),
    )


def on_device(
    inputs,
    w_query,
    b_query,
    w_key,
    w_value,
    b_value,
    w_out,
    b_out,
    first_gain,
    first_bias,
    w_hidden,
    b_hidden,
    w_down,
    b_down,
    second_gain,
    second_bias,
    cotangent,
):
    seq_count, part_len, width = inputs.shape
    per_micro = seq_count // MICRO
    row_count = per_micro * part_len
    head_cols = w_query.shape[1]
    hidden_cols = w_hidden.shape[1]
    factor = HEAD_DIM ** (-0.5)
    acc_query = jnp.zeros((width, head_cols), jnp.float32)
    acc_key = jnp.zeros((width, head_cols), jnp.float32)
    acc_value = jnp.zeros((width, head_cols), jnp.float32)
    acc_out = jnp.zeros((head_cols, width), jnp.float32)
    acc_hidden = jnp.zeros((width, hidden_cols), jnp.float32)
    acc_down = jnp.zeros((hidden_cols, width), jnp.float32)
    sum_b_query = jnp.zeros((head_cols,), jnp.float32)
    sum_b_value = jnp.zeros((head_cols,), jnp.float32)
    sum_b_out = jnp.zeros((width,), jnp.float32)
    sum_first_gain = jnp.zeros((width,), jnp.float32)
    sum_first_bias = jnp.zeros((width,), jnp.float32)
    sum_b_hidden = jnp.zeros((hidden_cols,), jnp.float32)
    sum_b_down = jnp.zeros((width,), jnp.float32)
    sum_second_gain = jnp.zeros((width,), jnp.float32)
    sum_second_bias = jnp.zeros((width,), jnp.float32)
    result_parts = []
    input_parts = []
    for batch_index in range(MICRO):
        full = (
            lax.all_gather(w_query, "shard", axis=0, tiled=True),
            lax.all_gather(w_key, "shard", axis=0, tiled=True),
            lax.all_gather(w_value, "shard", axis=0, tiled=True),
            lax.all_gather(w_out, "shard", axis=1, tiled=True),
            lax.all_gather(w_hidden, "shard", axis=0, tiled=True),
            lax.all_gather(w_down, "shard", axis=1, tiled=True),
        )
        full_query, full_key, full_value, full_out, full_hidden, full_down = full
        begin = batch_index * per_micro
        token_rows = inputs[begin : begin + per_micro].reshape(row_count, width)
        query_low = (
            jnp.dot(token_rows, full_query, preferred_element_type=jnp.float32) + b_query
        ).astype(jnp.bfloat16)
        key_low = jnp.dot(token_rows, full_key, preferred_element_type=jnp.float32).astype(
            jnp.bfloat16
        )
        value_low = (
            jnp.dot(token_rows, full_value, preferred_element_type=jnp.float32) + b_value
        ).astype(jnp.bfloat16)
        queries = query_low.reshape(per_micro, part_len, head_cols)
        local_keys = key_low.reshape(per_micro, part_len, head_cols)
        local_values = value_low.reshape(per_micro, part_len, head_cols)
        all_keys, all_values = (
            lax.all_gather(local_keys, "context", axis=1, tiled=True),
            lax.all_gather(local_values, "context", axis=1, tiled=True),
        )
        attended, totals = attend(queries, all_keys, all_values, factor)
        attended_rows = attended.reshape(row_count, head_cols)
        branch = lax.psum(
            jnp.dot(attended_rows, full_out, preferred_element_type=jnp.float32), "tensor"
        )
        first, normed_first, inverse_first = layer_norm(
            token_rows.astype(jnp.float32) + branch + b_out, first_gain, first_bias
        )
        first_low = first.astype(jnp.bfloat16)
        inner = jnp.dot(first_low, full_hidden, preferred_element_type=jnp.float32) + b_hidden
        activated, gelu_back = jax.vjp(gelu_exact, inner)
        activated_low = activated.astype(jnp.bfloat16)
        ffn = lax.psum(
            jnp.dot(activated_low, full_down, preferred_element_type=jnp.float32), "tensor"
        )
        result, normed_second, inverse_second = layer_norm(
            first + ffn + b_down, second_gain, second_bias
        )
        result_parts.append(result.astype(jnp.bfloat16).reshape(per_micro, part_len, width))
        grad_result = (
            cotangent[begin : begin + per_micro].reshape(row_count, width).astype(jnp.float32)
        )
        sum_second_gain = sum_second_gain + jnp.sum(grad_result * normed_second, axis=0)
        sum_second_bias = sum_second_bias + jnp.sum(grad_result, axis=0)
        grad_second = norm_back(grad_result, normed_second, inverse_second, second_gain)
        sum_b_down = sum_b_down + jnp.sum(grad_second, axis=0)
        grad_ffn = grad_second.astype(jnp.bfloat16)
        acc_down = acc_down + jnp.einsum(
            "rf,rd->fd", activated_low, grad_ffn, preferred_element_type=jnp.float32
        )
        grad_act = jnp.einsum("rd,fd->rf", grad_ffn, full_down, preferred_element_type=jnp.float32)
        grad_inner = gelu_back(grad_act)[0].astype(jnp.bfloat16)
        sum_b_hidden = sum_b_hidden + jnp.sum(grad_inner.astype(jnp.float32), axis=0)
        acc_hidden = acc_hidden + jnp.einsum(
            "rd,rf->df", first_low, grad_inner, preferred_element_type=jnp.float32
        )
        grad_first = grad_second + lax.psum(
            jnp.einsum("rf,df->rd", grad_inner, full_hidden, preferred_element_type=jnp.float32),
            "tensor",
        )
        sum_first_gain = sum_first_gain + jnp.sum(grad_first * normed_first, axis=0)
        sum_first_bias = sum_first_bias + jnp.sum(grad_first, axis=0)
        grad_pre_first = norm_back(grad_first, normed_first, inverse_first, first_gain)
        sum_b_out = sum_b_out + jnp.sum(grad_pre_first, axis=0)
        grad_attn = grad_pre_first.astype(jnp.bfloat16)
        acc_out = acc_out + jnp.einsum(
            "rh,rd->hd", attended_rows, grad_attn, preferred_element_type=jnp.float32
        )
        grad_heads = jnp.einsum(
            "rd,hd->rh", grad_attn, full_out, preferred_element_type=jnp.float32
        ).astype(jnp.bfloat16)
        grad_heads = grad_heads.reshape(per_micro, part_len, head_cols)
        grad_queries, grad_keys, grad_values = attend_back(
            queries, all_keys, all_values, grad_heads, totals, factor
        )
        own_keys, own_values = (
            lax.psum_scatter(grad_keys, "context", scatter_dimension=1, tiled=True),
            lax.psum_scatter(grad_values, "context", scatter_dimension=1, tiled=True),
        )
        grad_query_low = grad_queries.astype(jnp.bfloat16).reshape(row_count, head_cols)
        grad_key_low = own_keys.astype(jnp.bfloat16).reshape(row_count, head_cols)
        grad_value_low = own_values.astype(jnp.bfloat16).reshape(row_count, head_cols)
        sum_b_query = sum_b_query + jnp.sum(grad_query_low.astype(jnp.float32), axis=0)
        sum_b_value = sum_b_value + jnp.sum(grad_value_low.astype(jnp.float32), axis=0)
        acc_query = acc_query + jnp.einsum(
            "rd,rh->dh", token_rows, grad_query_low, preferred_element_type=jnp.float32
        )
        acc_key = acc_key + jnp.einsum(
            "rd,rh->dh", token_rows, grad_key_low, preferred_element_type=jnp.float32
        )
        acc_value = acc_value + jnp.einsum(
            "rd,rh->dh", token_rows, grad_value_low, preferred_element_type=jnp.float32
        )
        back_rows = (
            jnp.einsum("rh,dh->rd", grad_query_low, full_query, preferred_element_type=jnp.float32)
            + jnp.einsum("rh,dh->rd", grad_key_low, full_key, preferred_element_type=jnp.float32)
            + jnp.einsum(
                "rh,dh->rd", grad_value_low, full_value, preferred_element_type=jnp.float32
            )
        )
        grad_input = grad_pre_first + lax.psum(back_rows, "tensor")
        input_parts.append(grad_input.astype(jnp.bfloat16).reshape(per_micro, part_len, width))
    matrices = (acc_query, acc_key, acc_value, acc_out, acc_hidden, acc_down)
    owned = (
        lax.psum_scatter(
            matrices[0].astype(jnp.bfloat16), "shard", scatter_dimension=0, tiled=True
        ).astype(jnp.float32),
        lax.psum_scatter(
            matrices[1].astype(jnp.bfloat16), "shard", scatter_dimension=0, tiled=True
        ).astype(jnp.float32),
        lax.psum_scatter(
            matrices[2].astype(jnp.bfloat16), "shard", scatter_dimension=0, tiled=True
        ).astype(jnp.float32),
        lax.psum_scatter(
            matrices[3].astype(jnp.bfloat16), "shard", scatter_dimension=1, tiled=True
        ).astype(jnp.float32),
        lax.psum_scatter(
            matrices[4].astype(jnp.bfloat16), "shard", scatter_dimension=0, tiled=True
        ).astype(jnp.float32),
        lax.psum_scatter(
            matrices[5].astype(jnp.bfloat16), "shard", scatter_dimension=1, tiled=True
        ).astype(jnp.float32),
    )
    owned = (
        lax.psum(owned[0].astype(jnp.bfloat16), "context").astype(jnp.float32),
        lax.psum(owned[1].astype(jnp.bfloat16), "context").astype(jnp.float32),
        lax.psum(owned[2].astype(jnp.bfloat16), "context").astype(jnp.float32),
        lax.psum(owned[3].astype(jnp.bfloat16), "context").astype(jnp.float32),
        lax.psum(owned[4].astype(jnp.bfloat16), "context").astype(jnp.float32),
        lax.psum(owned[5].astype(jnp.bfloat16), "context").astype(jnp.float32),
    )
    vectors = lax.psum(
        (
            sum_b_query,
            sum_b_value,
            sum_b_out,
            sum_first_gain,
            sum_first_bias,
            sum_b_hidden,
            sum_b_down,
            sum_second_gain,
            sum_second_bias,
        ),
        ("shard", "context"),
    )
    return (
        jnp.concatenate(result_parts, axis=0),
        jnp.concatenate(input_parts, axis=0),
        owned[0],
        vectors[0],
        owned[1],
        owned[2],
        vectors[1],
        owned[3],
        vectors[2],
        vectors[3],
        vectors[4],
        owned[4],
        vectors[5],
        owned[5],
        vectors[6],
        vectors[7],
        vectors[8],
    )


def solution(mesh):
    return jax.shard_map(
        on_device,
        mesh=mesh,
        in_specs=(
            P("shard", "context", None),
            P("shard", "tensor"),
            P("tensor"),
            P("shard", "tensor"),
            P("shard", "tensor"),
            P("tensor"),
            P("tensor", "shard"),
            P(),
            P(),
            P(),
            P("shard", "tensor"),
            P("tensor"),
            P("tensor", "shard"),
            P(),
            P(),
            P(),
            P("shard", "context", None),
        ),
        out_specs=(
            P("shard", "context", None),
            P("shard", "context", None),
            P("shard", "tensor"),
            P("tensor"),
            P("shard", "tensor"),
            P("shard", "tensor"),
            P("tensor"),
            P("tensor", "shard"),
            P(),
            P(),
            P(),
            P("shard", "tensor"),
            P("tensor"),
            P("tensor", "shard"),
            P(),
            P(),
            P(),
        ),
        check_vma=False,
    )
```

profile of v0, /device:TPU:0, one launch (start us, length us, event | category | flops | bytes accessed | tf_op | source)
XLA Modules:
  0.0 1056.1 jit_solution(5960588439616806110)
XLA Ops:
  8.1 7.7 all_gather.48
  19.7 5.8 all_gather.49
  26.8 5.8 all_gather.51
  33.9 18.1 %all-gather.4 = bf16[2048,192]{0,1:T(8,128)(2,1)S(1)} all-gather(bf16[512,192]{0,1:T(8,128)(2,1)S(1)} %convolution_convert_fusion.3), channel_id=6, replica_groups=mesh['shard'=2,'context'=4,'tensor'=4] {'context'}, dimensions={0}, use_global_device_ids=true | all-gather | bytes 983040 | tf_op jit(solution)/shard_map/all_gather | solution.py:169
  54.5 17.6 %all-gather.2 = bf16[2048,192]{0,1:T(8,128)(2,1)S(1)} all-gather(bf16[512,192]{0,1:T(8,128)(2,1)S(1)} %convolution_convert_fusion.4), channel_id=4, replica_groups=mesh['shard'=2,'context'=4,'tensor'=4] {'context'}, dimensions={0}, use_global_device_ids=true | all-gather | bytes 983040 | tf_op jit(solution)/shard_map/all_gather | solution.py:169
  74.5 15.7 %all-gather = bf16[2048,192]{0,1:T(8,128)(2,1)S(1)} all-gather(bf16[512,192]{0,1:T(8,128)(2,1)S(1)} %convolution_convert_fusion.5), channel_id=2, replica_groups=mesh['shard'=2,'context'=4,'tensor'=4] {'context'}, dimensions={0}, use_global_device_ids=true | all-gather | bytes 983040 | tf_op jit(solution)/shard_map/all_gather | solution.py:169
  93.0 5.8 all_gather.53
  98.8 17.9 %all-gather.1 = bf16[2048,192]{0,1:T(8,128)(2,1)S(1)} all-gather(bf16[512,192]{0,1:T(8,128)(2,1)S(1)} %fusion.71), channel_id=3, replica_groups=mesh['shard'=2,'context'=4,'tensor'=4] {'context'}, dimensions={0}, use_global_device_ids=true | all-gather | bytes 983040 | tf_op jit(solution)/shard_map/all_gather | solution.py:170
  116.7 19.4 %all-gather.3 = bf16[2048,192]{0,1:T(8,128)(2,1)S(1)} all-gather(bf16[512,192]{0,1:T(8,128)(2,1)S(1)} %fusion.73), channel_id=5, replica_groups=mesh['shard'=2,'context'=4,'tensor'=4] {'context'}, dimensions={0}, use_global_device_ids=true | all-gather | bytes 983040 | tf_op jit(solution)/shard_map/all_gather | solution.py:170
  136.1 15.8 %all-gather.5 = bf16[2048,192]{0,1:T(8,128)(2,1)S(1)} all-gather(bf16[512,192]{0,1:T(8,128)(2,1)S(1)} %fusion.75), channel_id=7, replica_groups=mesh['shard'=2,'context'=4,'tensor'=4] {'context'}, dimensions={0}, use_global_device_ids=true | all-gather | bytes 983040 | tf_op jit(solution)/shard_map/all_gather | solution.py:170
  174.4 93.1 %all-reduce.18.cloned.1.call-done = (f32[512,768]{1,0:T(8,128)}, f32[512,768]{1,0:T(8,128)}, f32[512,768]{1,0:T(8,128)}) async-done(((f32[512,768]{1,0:T(8,128)}, f32[512,768]{1,0:T(8,128)}, f32[512,768]{1,0:T(8,128)}), (f32[512,768]{1,0:T(8,128)}, f32[512,768]{1,0:T(8,128)}, f32[512,768]{1,0:T(8,128)})) %all-reduce.18.cloned.1.call-update) | async-done | bytes 4718608 | tf_op jit(solution)/shard_map/psum | solution.py:174
  272.5 6.9 multiply_convert_fusion.10
  279.4 5.6 multiply_convert_fusion.9
  290.6 5.5 multiply_convert_fusion.11
  299.2 94.5 %all-reduce.16.cloned.1.call-done = (f32[512,768]{1,0:T(8,128)}, f32[512,768]{1,0:T(8,128)}, f32[512,768]{1,0:T(8,128)}) async-done(((f32[512,768]{1,0:T(8,128)}, f32[512,768]{1,0:T(8,128)}, f32[512,768]{1,0:T(8,128)}), (f32[512,768]{1,0:T(8,128)}, f32[512,768]{1,0:T(8,128)}, f32[512,768]{1,0:T(8,128)})) %all-reduce.16.cloned.1.call-update) | async-done | bytes 4718608 | tf_op jit(solution)/shard_map/psum | solution.py:184
  421.8 94.4 %all-reduce.14.cloned.1.call-done = (f32[512,768]{1,0:T(8,128)}, f32[512,768]{1,0:T(8,128)}, f32[512,768]{1,0:T(8,128)}) async-done(((f32[512,768]{1,0:T(8,128)}, f32[512,768]{1,0:T(8,128)}, f32[512,768]{1,0:T(8,128)}), (f32[512,768]{1,0:T(8,128)}, f32[512,768]{1,0:T(8,128)}, f32[512,768]{1,0:T(8,128)})) %all-reduce.14.cloned.1.call-update) | async-done | bytes 4718608 | tf_op jit(solution)/shard_map/psum | solution.py:208
  520.4 5.2 fusion.253
  555.8 5.3 multiply_reduce_fusion.6
  565.2 4.6 multiply_convert_fusion.6
  582.3 5.3 multiply_reduce_fusion.3
  591.9 4.6 multiply_convert_fusion.3
  679.6 34.8 %reduce-scatter.27.cloned.1.call-done = f32[1,512,192]{1,2,0:T(8,128)} async-done(((f32[1,2048,192]{1,2,0:T(8,128)}), f32[1,512,192]{1,2,0:T(8,128)}) %reduce-scatter.27.cloned.1.call-update) | async-done | bytes 393232 | tf_op jit(solution)/shard_map/reduce_scatter | solution.py:228
  716.8 34.0 %reduce-scatter.31.cloned.1.call-done = f32[1,512,192]{1,2,0:T(8,128)} async-done(((f32[1,2048,192]{1,2,0:T(8,128)}), f32[1,512,192]{1,2,0:T(8,128)}) %reduce-scatter.31.cloned.1.call-update) | async-done | bytes 393232 | tf_op jit(solution)/shard_map/reduce_scatter | solution.py:228
  760.4 13.6 %reduce-scatter.45.cloned.1.call-done = bf16[384,768]{1,0:T(8,128)(2,1)} async-done(((bf16[768,768]{1,0:T(8,128)(2,1)}), bf16[384,768]{1,0:T(8,128)(2,1)}) %reduce-scatter.45.cloned.1.call-update) | async-done | bytes 589840
  778.6 10.8 %reduce-scatter.43.cloned.1.call-done = bf16[384,192]{1,0:T(8,128)(2,1)} async-done(((bf16[768,192]{1,0:T(8,128)(2,1)}), bf16[384,192]{1,0:T(8,128)(2,1)}) %reduce-scatter.43.cloned.1.call-update) | async-done | bytes 147472
  791.2 14.0 %reduce-scatter.37.cloned.1.call-done = bf16[384,192]{1,0:T(8,128)(2,1)} async-done(((bf16[768,192]{1,0:T(8,128)(2,1)}), bf16[384,192]{1,0:T(8,128)(2,1)}) %reduce-scatter.37.cloned.1.call-update) | async-done | bytes 147472
  806.9 13.7 %reduce-scatter.41.cloned.1.call-done = bf16[384,192]{1,0:T(8,128)(2,1)} async-done(((bf16[768,192]{1,0:T(8,128)(2,1)}), bf16[384,192]{1,0:T(8,128)(2,1)}) %reduce-scatter.41.cloned.1.call-update) | async-done | bytes 147472
  822.3 13.4 %reduce-scatter.39.cloned.1.call-done = bf16[384,192]{1,0:T(8,128)(2,1)} async-done(((bf16[768,192]{1,0:T(8,128)(2,1)}), bf16[384,192]{1,0:T(8,128)(2,1)}) %reduce-scatter.39.cloned.1.call-update) | async-done | bytes 147472
  837.4 22.9 %reduce-scatter.35.cloned.1.call-done = bf16[384,768]{1,0:T(8,128)(2,1)} async-done(((bf16[768,768]{1,0:T(8,128)(2,1)}), bf16[384,768]{1,0:T(8,128)(2,1)}) %reduce-scatter.35.cloned.1.call-update) | async-done | bytes 589840 | tf_op jit(solution)/shard_map/reduce_scatter | solution.py:268
  874.0 38.7 %all-reduce = (f32[192]{0:T(256)}, f32[192]{0:T(256)}, f32[768]{0:T(1024)}, f32[768]{0:T(1024)}, f32[768]{0:T(1024)}, /*index=5*/f32[768]{0:T(1024)}, f32[768]{0:T(1024)}, f32[768]{0:T(1024)}, f32[768]{0:T(1024)}) all-reduce(f32[192]{0:T(256)S(1)} %add_add_fusion.17, ...), channel_id=1, replica_groups=mesh['shard'=2,'context'=4,'tensor'=4] {'shard','context'}, use_global_device_ids=true, to_apply=%region_74.0 | all-reduce | flops 5760 | bytes 46080 | tf_op jit(solution)/shard_map/psum | solution.py:283
  912.7 30.0 %all-reduce.20.cloned.1.call-done = (bf16[384,192]{0,1:T(8,128)(2,1)}, bf16[384,192]{0,1:T(8,128)(2,1)}, bf16[384,192]{0,1:T(8,128)(2,1)}, bf16[192,384]{1,0:T(8...) async-done(((bf16[384,192]{0,1:T(8,128)(2,1)}, bf16[384,192]{0,1:T(8,128)(2,1)}, bf16[384,192]{0,1:T(8,128)(2,1)}, bf16[192,384]{1,0:T(8,128)(2,1)}, ...) | async-done | bytes 1769488 | tf_op jit(solution)/shard_map/psum | solution.py:276
  949.3 89.8 %all-reduce.12.cloned.1.call-done = (f32[512,768]{1,0:T(8,128)}, f32[512,768]{1,0:T(8,128)}, f32[512,768]{1,0:T(8,128)}) async-done(((f32[512,768]{1,0:T(8,128)}, f32[512,768]{1,0:T(8,128)}, f32[512,768]{1,0:T(8,128)}), (f32[512,768]{1,0:T(8,128)}, f32[512,768]{1,0:T(8,128)}, f32[512,768]{1,0:T(8,128)})) %all-reduce.12.cloned.1.call-update) | async-done | bytes 4718608 | tf_op jit(solution)/shard_map/psum | solution.py:252
  (684 shorter events, 267.0 us)
Async XLA Ops:
  8.0 259.5 %all-reduce.18.cloned.1.call-start = ((), (), s32[]{:S(2)}) async-start(), calls=%async_computation.29 | async-start | bytes 9437184 | tf_op jit(solution)/shard_map/psum | solution.py:174
  52.8 100.8 %copy-start.6 = (f32[512,2048]{1,0:T(8,128)}, f32[512,2048]{1,0:T(8,128)S(1)}, u32[]{:S(2)}) copy-start(f32[512,2048]{1,0:T(8,128)S(1)} %get-tuple-element.131) | copy-start | bytes 12582916
  53.7 100.9 %copy-start.3 = (f32[512,2048]{1,0:T(8,128)}, f32[512,2048]{1,0:T(8,128)S(1)}, u32[]{:S(2)}) copy-start(f32[512,2048]{1,0:T(8,128)S(1)} %get-tuple-element.133) | copy-start | bytes 12582916
  54.5 101.9 %copy-start = (f32[512,2048]{1,0:T(8,128)}, f32[512,2048]{1,0:T(8,128)S(1)}, u32[]{:S(2)}) copy-start(f32[512,2048]{1,0:T(8,128)S(1)} %get-tuple-element.135) | copy-start | bytes 12582916
  74.5 87.2 %copy-start.8 = (f32[512,2048]{1,0:T(8,128)}, f32[512,2048]{1,0:T(8,128)S(1)}, u32[]{:S(2)}) copy-start(f32[512,2048]{1,0:T(8,128)S(1)} %get-tuple-element.141) | copy-start | bytes 12582916
  153.6 397.4 %copy-start.165 = (f32[512]{0:T(512)}, f32[512]{0:T(512)S(1)}, u32[]{:S(2)}) copy-start(f32[512]{0:T(512)S(1)} %log_add_fusion.1) | copy-start | bytes 6148
  156.3 395.8 %copy-start.163 = (f32[512]{0:T(512)}, f32[512]{0:T(512)S(1)}, u32[]{:S(2)}) copy-start(f32[512]{0:T(512)S(1)} %log_add_fusion.2) | copy-start | bytes 6148
  173.2 94.4 %copy-start.191 = (f32[768]{0:T(1024)S(1)}, f32[768]{0:T(1024)}, u32[]{:S(2)}) copy-start(f32[768]{0:T(1024)} %param.24) | copy-start | bytes 9220
  173.2 99.3 %all-gather.9.cloned.1.call-start = ((), (), s32[]{:S(2)}) async-start(), calls=%async_computation.12 | async-start | bytes 1769472 | tf_op jit(solution)/shard_map/all_gather | solution.py:150
  173.8 111.3 %all-gather.11.cloned.1.call-start = ((), (), s32[]{:S(2)}) async-start(), calls=%async_computation.13 | async-start | bytes 1769472 | tf_op jit(solution)/shard_map/all_gather | solution.py:151
  174.4 219.3 %all-reduce.16.cloned.1.call-start = ((), (), s32[]{:S(2)}) async-start(), calls=%async_computation.28 | async-start | bytes 9437184 | tf_op jit(solution)/shard_map/psum | solution.py:184
  271.3 261.6 %copy-start.161 = (f32[512]{0:T(512)}, f32[512]{0:T(512)S(1)}, u32[]{:S(2)}) copy-start(f32[512]{0:T(512)S(1)} %broadcast_multiply_fusion.15) | copy-start | bytes 6148
  271.7 248.5 %copy-start.168 = (f32[512]{0:T(512)}, f32[512]{0:T(512)S(1)}, u32[]{:S(2)}) copy-start(f32[512]{0:T(512)S(1)} %add_rsqrt_fusion.5) | copy-start | bytes 6148
  272.5 260.5 %copy-start.170 = (f32[512]{0:T(512)}, f32[512]{0:T(512)S(1)}, u32[]{:S(2)}) copy-start(f32[512]{0:T(512)S(1)} %add_rsqrt_fusion.3) | copy-start | bytes 6148
  299.0 94.7 %copy-start.192 = (f32[768]{0:T(1024)S(1)}, f32[768]{0:T(1024)}, u32[]{:S(2)}) copy-start(f32[768]{0:T(1024)} %param.30) | copy-start | bytes 9220
  299.0 217.2 %all-reduce.14.cloned.1.call-start = ((), (), s32[]{:S(2)}) async-start(), calls=%async_computation.27 | async-start | bytes 9437184 | tf_op jit(solution)/shard_map/psum | solution.py:208
  421.5 246.6 %reduce-scatter.25.cloned.1.call-start = ((), (), s32[]{:S(2)}) async-start(), calls=%async_computation.15 | async-start | bytes 1966080 | tf_op jit(solution)/shard_map/reduce_scatter | solution.py:229
  532.8 136.9 %reduce-scatter.29.cloned.1.call-start = ((), (), s32[]{:S(2)}) async-start(), calls=%async_computation.17 | async-start | bytes 1966080 | tf_op jit(solution)/shard_map/reduce_scatter | solution.py:229
  545.4 126.0 %reduce-scatter.33.cloned.1.call-start = ((), (), s32[]{:S(2)}) async-start(), calls=%async_computation.19 | async-start | bytes 1966080 | tf_op jit(solution)/shard_map/reduce_scatter | solution.py:229
  565.1 112.9 %reduce-scatter.23.cloned.1.call-start = ((), (), s32[]{:S(2)}) async-start(), calls=%async_computation.14 | async-start | bytes 1966080 | tf_op jit(solution)/shard_map/reduce_scatter | solution.py:228
  591.7 122.7 %reduce-scatter.27.cloned.1.call-start = ((), (), s32[]{:S(2)}) async-start(), calls=%async_computation.16 | async-start | bytes 1966080 | tf_op jit(solution)/shard_map/reduce_scatter | solution.py:228
  615.0 135.8 %reduce-scatter.31.cloned.1.call-start = ((), (), s32[]{:S(2)}) async-start(), calls=%async_computation.18 | async-start | bytes 1966080 | tf_op jit(solution)/shard_map/reduce_scatter | solution.py:228
  629.9 144.1 %reduce-scatter.45.cloned.1.call-start = ((), (), s32[]{:S(2)}) async-start(), calls=%async_computation.25 | async-start | bytes 1769472
  642.2 147.2 %reduce-scatter.43.cloned.1.call-start = ((), (), s32[]{:S(2)}) async-start(), calls=%async_computation.24 | async-start | bytes 589824
  659.1 119.1 %copy-start.100 = (bf16[512,64]{0,1:T(8,128)(2,1)}, bf16[512,64]{0,1:T(8,128)(2,1)S(1)}, u32[]{:S(2)}) copy-start(bf16[512,64]{0,1:T(8,128)(2,1)S(1)} %fusion.90) | copy-start | bytes 196612
  661.5 143.7 %reduce-scatter.37.cloned.1.call-start = ((), (), s32[]{:S(2)}) async-start(), calls=%async_computation.21 | async-start | bytes 589824
  668.0 152.5 %reduce-scatter.41.cloned.1.call-start = ((), (), s32[]{:S(2)}) async-start(), calls=%async_computation.23 | async-start | bytes 589824
  673.9 161.8 %reduce-scatter.39.cloned.1.call-start = ((), (), s32[]{:S(2)}) async-start(), calls=%async_computation.22 | async-start | bytes 589824
  753.5 106.8 %reduce-scatter.35.cloned.1.call-start = ((), (), s32[]{:S(2)}) async-start(), calls=%async_computation.20 | async-start | bytes 1769472 | tf_op jit(solution)/shard_map/reduce_scatter | solution.py:268
  758.1 184.6 %all-reduce.20.cloned.1.call-start = ((), (), s32[]{:S(2)}) async-start(), calls=%async_computation.30 | async-start | bytes 3538944 | tf_op jit(solution)/shard_map/psum | solution.py:276
  860.3 178.7 %all-reduce.12.cloned.1.call-start = ((), (), s32[]{:S(2)}) async-start(), calls=%async_computation.26 | async-start | bytes 9437184 | tf_op jit(solution)/shard_map/psum | solution.py:252
  873.5 165.6 %copy-start.32 = (f32[512,768]{1,0:T(8,128)S(1)}, f32[512,768]{1,0:T(8,128)}, u32[]{:S(2)}) copy-start(f32[512,768]{1,0:T(8,128)} %copy-done.31) | copy-start | bytes 4718596
  (199 other events, 1429.4 us)
Sparse Core Ops, SparseCore 0:
  173.3 94.1 all-reduce.17
  299.1 94.5 all-reduce.15
  421.6 94.5 all-reduce.13
Sparse Core Ops, SparseCore 1:
  175.2 22.4 all-gather.8
  199.1 22.6 all-gather.10
  532.9 35.4 reduce-scatter.24
  570.7 34.1 reduce-scatter.28
  607.2 34.1 reduce-scatter.32
  643.8 34.2 reduce-scatter.22
  680.2 34.1 reduce-scatter.26
  716.5 34.1 reduce-scatter.30
  753.4 20.5 reduce-scatter.44
  776.4 13.0 reduce-scatter.42
  792.1 13.0 reduce-scatter.36
  807.5 13.0 reduce-scatter.40
  822.7 13.0 reduce-scatter.38
  838.6 21.6 reduce-scatter.34
  864.3 78.3 all-reduce.19
  946.0 93.0 all-reduce.11
where the time goes:
time: 1060 us
  waiting for transfers between devices  564 us (53%)
  blocking collectives  168 us (16%)
  matrix products  167 us (16%)
  other arithmetic  80.6 us (8%)
  local copies, waits for them, and re-layouts  54.3 us (5%)
  between operations  18.8 us (2%)
    psum x1, waiting for transfers between devices, on_device(): lax.psum(jnp.dot(activated_low, full_down, preferred_element_type=jnp.flo...  94.5 us
    psum x1, waiting for transfers between devices, on_device(): lax.psum(jnp.einsum('rf,df->rd', grad_inner, full_hidden, preferred_eleme...  94.4 us
    psum x1, waiting for transfers between devices, on_device(): lax.psum(jnp.dot(attended_rows, full_out, preferred_element_type=jnp.floa...  93.1 us
    psum x1, waiting for transfers between devices, on_device(): grad_input = grad_pre_first + lax.psum(back_rows, 'tensor')  89.8 us
    reduce_scatter x3, waiting for transfers between devices, on_device(): lax.psum_scatter(grad_keys, 'context', scatter_dimension=1, tiled=True)  72.8 us
    unnamed x24, waiting for transfers between devices  66.9 us
    unnamed x434, local copies, waits for them, and re-layouts  54.3 us
    all_gather x3, blocking collectives, on_device(): lax.all_gather(local_values, 'context', axis=1, tiled=True)  53.1 us
  transfers between devices with their start and end apart: 19, of which 14 were waited for; matrix products, arithmetic and copies ran while one was open for 16% of the time, Pallas kernels for 0%

commit v1 on v0

--- a/solution.py
+++ b/solution.py
@@ -6,6 +6,24 @@
 HEAD_DIM = 64
 MICRO = 3
 EPSILON = 1e-05
+
+
+def ring_gather(value, axis, dim):
+    ways, here, step = (lax.axis_size(axis), lax.axis_index(axis), value.shape[dim])
+    shape = [n * ways if d == dim else n for d, n in enumerate(value.shape)]
+    full = lax.dynamic_update_slice_in_dim(
+        jnp.zeros(shape, value.dtype), value, here * step, axis=dim
+    )
+    going_up = going_down = value
+    for far in range(1, ways // 2 + 1):
+        going_up = lax.ppermute(going_up, axis, [(d, (d + 1) % ways) for d in range(ways)])
+        full = lax.dynamic_update_slice_in_dim(full, going_up, (here - far) % ways * step, axis=dim)
+        if 2 * far < ways:
+            going_down = lax.ppermute(going_down, axis, [(d, (d - 1) % ways) for d in range(ways)])
+            full = lax.dynamic_update_slice_in_dim(
+                full, going_down, (here + far) % ways * step, axis=dim
+            )
+    return full
 
 
 def layer_norm(values, gain, bias):
@@ -167,7 +185,7 @@
         local_values = value_low.reshape(per_micro, part_len, head_cols)
         all_keys, all_values = (
             lax.all_gather(local_keys, "context", axis=1, tiled=True),
-            lax.all_gather(local_values, "context", axis=1, tiled=True),
+            ring_gather(local_values, "context", 1),
         )
         attended, totals = attend(queries, all_keys, all_values, factor)
         attended_rows = attended.reshape(row_count, head_cols)

time: 1060 us -> 948 us (0.89)
  waiting for transfers between devices: 564 us -> 476 us
  blocking collectives: 168 us -> 116 us
  local copies, waits for them, and re-layouts: 54.3 us -> 68 us
  starting transfers between devices: 2.54 us -> 14.4 us
    psum x1, waiting for transfers between devices: 89.8 us -> 0.01 us  [on_device(): grad_input = grad_pre_first + lax.psum(back_rows, 'tensor')]
    all_gather x3 -> x0, blocking collectives: 53.1 us -> none  [on_device(): lax.all_gather(local_values, 'context', axis=1, tiled=True)]
    ppermute x0 -> x9, starting transfers between devices: none -> 11.4 us  [the longest x3 7.91 us: ring_gather(): lax.ppermute(going_down, axis, [(d, (d - 1) % ways) for d in range(ways)])]
    unnamed x24, waiting for transfers between devices: 66.9 us -> 55.5 us
    unnamed x434 -> x448, local copies, waits for them, and re-layouts: 54.3 us -> 64.8 us
  transfers between devices with their start and end apart: 19 -> 28, of which waited for: 14 -> 14; matrix products, arithmetic and copies ran while one was open for 16% -> 21% of each run, Pallas kernels for 0% -> 0%
where the time goes in v1:
time: 948 us; the launch traced here: 940 us
  waiting for transfers between devices  476 us (50%)
  matrix products  168 us (18%)
  blocking collectives  116 us (12%)
  other arithmetic  79.2 us (8%)
  local copies, waits for them, and re-layouts  68 us (7%)
  between operations  18.9 us (2%)
  starting transfers between devices  14.4 us (2%)
    psum x1, waiting for transfers between devices, on_device(): lax.psum(jnp.dot(activated_low, full_down, preferred_element_type=jnp.flo...  94.5 us
    psum x1, waiting for transfers between devices, on_device(): lax.psum(jnp.einsum('rf,df->rd', grad_inner, full_hidden, preferred_eleme...  94.4 us
    psum x1, waiting for transfers between devices, on_device(): lax.psum(jnp.dot(attended_rows, full_out, preferred_element_type=jnp.floa...  92.3 us
    reduce_scatter x3, waiting for transfers between devices, on_device(): lax.psum_scatter(grad_keys, 'context', scatter_dimension=1, tiled=True)  72.4 us
    unnamed x448, local copies, waits for them, and re-layouts  64.8 us
    unnamed x24, waiting for transfers between devices  55.5 us
    all_gather x3, blocking collectives, on_device(): lax.all_gather(local_keys, 'context', axis=1, tiled=True)  51.8 us
    psum x1, waiting for transfers between devices, on_device(): lax.psum(owned[0].astype(jnp.bfloat16), 'context').astype(jnp.float32)  38.7 us
  transfers between devices with their start and end apart: 28, of which 14 were waited for; matrix products, arithmetic and copies ran while one was open for 21% of the time, Pallas kernels for 0%

profile of v1, /device:TPU:0, one launch (start us, length us, event | category | flops | bytes accessed | tf_op | source)
XLA Modules:
  0.0 939.8 jit_solution(10561275189795145511)
XLA Ops:
  8.1 7.7 all_gather.42
  28.4 5.8 all_gather.18
  35.6 5.8 all_gather.19
  42.6 18.0 %all-gather.2 = bf16[2048,192]{0,1:T(8,128)(2,1)S(1)} all-gather(bf16[512,192]{0,1:T(8,128)(2,1)S(1)} %convolution_convert_fusion.3), channel_id=4, replica_groups=mesh['shard'=2,'context'=4,'tensor'=4] {'context'}, dimensions={0}, use_global_device_ids=true | all-gather | bytes 983040 | tf_op jit(solution)/shard_map/all_gather | solution.py:187
  63.1 17.9 %all-gather.1 = bf16[2048,192]{0,1:T(8,128)(2,1)S(1)} all-gather(bf16[512,192]{0,1:T(8,128)(2,1)S(1)} %convolution_convert_fusion.4), channel_id=3, replica_groups=mesh['shard'=2,'context'=4,'tensor'=4] {'context'}, dimensions={0}, use_global_device_ids=true | all-gather | bytes 983040 | tf_op jit(solution)/shard_map/all_gather | solution.py:187
  83.5 15.9 %all-gather = bf16[2048,192]{0,1:T(8,128)(2,1)S(1)} all-gather(bf16[512,192]{0,1:T(8,128)(2,1)S(1)} %convolution_convert_fusion.5), channel_id=2, replica_groups=mesh['shard'=2,'context'=4,'tensor'=4] {'context'}, dimensions={0}, use_global_device_ids=true | all-gather | bytes 983040 | tf_op jit(solution)/shard_map/all_gather | solution.py:187
  109.6 5.8 all_gather.43
  122.2 4.9 collective-permute-done.8
  154.4 92.3 %all-reduce.18.cloned.1.call-done = (f32[512,768]{1,0:T(8,128)}, f32[512,768]{1,0:T(8,128)}, f32[512,768]{1,0:T(8,128)}) async-done(((f32[512,768]{1,0:T(8,128)}, f32[512,768]{1,0:T(8,128)}, f32[512,768]{1,0:T(8,128)}), (f32[512,768]{1,0:T(8,128)}, f32[512,768]{1,0:T(8,128)}, f32[512,768]{1,0:T(8,128)})) %all-reduce.18.cloned.1.call-update) | async-done | bytes 4718608 | tf_op jit(solution)/shard_map/psum | solution.py:192
  251.7 6.9 multiply_convert_fusion.10
  258.5 5.6 multiply_convert_fusion.9
  269.7 5.4 multiply_convert_fusion.11
  278.3 94.5 %all-reduce.16.cloned.1.call-done = (f32[512,768]{1,0:T(8,128)}, f32[512,768]{1,0:T(8,128)}, f32[512,768]{1,0:T(8,128)}) async-done(((f32[512,768]{1,0:T(8,128)}, f32[512,768]{1,0:T(8,128)}, f32[512,768]{1,0:T(8,128)}), (f32[512,768]{1,0:T(8,128)}, f32[512,768]{1,0:T(8,128)}, f32[512,768]{1,0:T(8,128)})) %all-reduce.16.cloned.1.call-update) | async-done | bytes 4718608 | tf_op jit(solution)/shard_map/psum | solution.py:202
  400.9 94.4 %all-reduce.14.cloned.1.call-done = (f32[512,768]{1,0:T(8,128)}, f32[512,768]{1,0:T(8,128)}, f32[512,768]{1,0:T(8,128)}) async-done(((f32[512,768]{1,0:T(8,128)}, f32[512,768]{1,0:T(8,128)}, f32[512,768]{1,0:T(8,128)}), (f32[512,768]{1,0:T(8,128)}, f32[512,768]{1,0:T(8,128)}, f32[512,768]{1,0:T(8,128)})) %all-reduce.14.cloned.1.call-update) | async-done | bytes 4718608 | tf_op jit(solution)/shard_map/psum | solution.py:226
  495.3 3.9 multiply_reduce_fusion.20
  499.6 5.2 fusion.256
  512.1 4.1 fusion.255
  534.9 5.3 multiply_reduce_fusion.6
  540.2 4.0 multiply_reduce_fusion.7
  544.4 4.6 multiply_convert_fusion.6
  561.6 5.3 multiply_reduce_fusion.3
  566.9 4.1 multiply_reduce_fusion.4
  571.3 4.6 multiply_convert_fusion.3
  658.7 34.8 %reduce-scatter.27.cloned.1.call-done = f32[1,512,192]{1,2,0:T(8,128)} async-done(((f32[1,2048,192]{1,2,0:T(8,128)}), f32[1,512,192]{1,2,0:T(8,128)}) %reduce-scatter.27.cloned.1.call-update) | async-done | bytes 393232 | tf_op jit(solution)/shard_map/reduce_scatter | solution.py:246
  695.9 34.0 %reduce-scatter.31.cloned.1.call-done = f32[1,512,192]{1,2,0:T(8,128)} async-done(((f32[1,2048,192]{1,2,0:T(8,128)}), f32[1,512,192]{1,2,0:T(8,128)}) %reduce-scatter.31.cloned.1.call-update) | async-done | bytes 393232 | tf_op jit(solution)/shard_map/reduce_scatter | solution.py:246
  755.8 12.7 %reduce-scatter.43.cloned.1.call-done = bf16[384,192]{1,0:T(8,128)(2,1)} async-done(((bf16[768,192]{1,0:T(8,128)(2,1)}), bf16[384,192]{1,0:T(8,128)(2,1)}) %reduce-scatter.43.cloned.1.call-update) | async-done | bytes 147472
  770.3 13.5 %reduce-scatter.37.cloned.1.call-done = bf16[384,192]{1,0:T(8,128)(2,1)} async-done(((bf16[768,192]{1,0:T(8,128)(2,1)}), bf16[384,192]{1,0:T(8,128)(2,1)}) %reduce-scatter.37.cloned.1.call-update) | async-done | bytes 147472
  785.5 13.7 %reduce-scatter.41.cloned.1.call-done = bf16[384,192]{1,0:T(8,128)(2,1)} async-done(((bf16[768,192]{1,0:T(8,128)(2,1)}), bf16[384,192]{1,0:T(8,128)(2,1)}) %reduce-scatter.41.cloned.1.call-update) | async-done | bytes 147472
  801.0 13.5 %reduce-scatter.39.cloned.1.call-done = bf16[384,192]{1,0:T(8,128)(2,1)} async-done(((bf16[768,192]{1,0:T(8,128)(2,1)}), bf16[384,192]{1,0:T(8,128)(2,1)}) %reduce-scatter.39.cloned.1.call-update) | async-done | bytes 147472
  816.1 22.9 %reduce-scatter.35.cloned.1.call-done = bf16[384,768]{1,0:T(8,128)(2,1)} async-done(((bf16[768,768]{1,0:T(8,128)(2,1)}), bf16[384,768]{1,0:T(8,128)(2,1)}) %reduce-scatter.35.cloned.1.call-update) | async-done | bytes 589840 | tf_op jit(solution)/shard_map/reduce_scatter | solution.py:286
  839.5 38.7 %all-reduce = (f32[192]{0:T(256)}, f32[192]{0:T(256)}, f32[768]{0:T(1024)}, f32[768]{0:T(1024)}, f32[768]{0:T(1024)}, /*index=5*/f32[768]{0:T(1024)}, f32[768]{0:T(1024)}, f32[768]{0:T(1024)}, f32[768]{0:T(1024)}) all-reduce(f32[192]{0:T(256)S(1)} %add_add_fusion.17, ...), channel_id=1, replica_groups=mesh['shard'=2,'context'=4,'tensor'=4] {'shard','context'}, use_global_device_ids=true, to_apply=%region_74.75 | all-reduce | flops 5760 | bytes 46080 | tf_op jit(solution)/shard_map/psum | solution.py:301
  884.4 38.7 %all-reduce.20.cloned.1.call-done = (bf16[384,192]{0,1:T(8,128)(2,1)}, bf16[384,192]{0,1:T(8,128)(2,1)}, bf16[384,192]{0,1:T(8,128)(2,1)}, bf16[192,384]{1,0:T(8...) async-done(((bf16[384,192]{0,1:T(8,128)(2,1)}, bf16[384,192]{0,1:T(8,128)(2,1)}, bf16[384,192]{0,1:T(8,128)(2,1)}, bf16[192,384]{1,0:T(8,128)(2,1)}, ...) | async-done | bytes 1769488 | tf_op jit(solution)/shard_map/psum | solution.py:294
  (725 shorter events, 276.2 us)
Async XLA Ops:
  8.0 238.6 %all-reduce.18.cloned.1.call-start = ((), (), s32[]{:S(2)}) async-start(), calls=%async_computation.29 | async-start | bytes 9437184 | tf_op jit(solution)/shard_map/psum | solution.py:192
  18.3 97.2 %collective-permute-start.3 = (bf16[1,512,192]{1,2,0:T(8,128)(2,1)}, bf16[1,512,192]{1,2,0:T(8,128)(2,1)S(1)}, u32[]{:S(2)}, u32[]{:S(2)}) collective-permute-start(bf16[1,512,192]{1,2,0:T(8,128)(2,1)} %get-tuple-element.139), channel_id=1, source_target_pairs={{0,4},{4,8},{8,12},{12,0},{1,5},{5,9},{9,13},{13,1},{2,6},{6,10},{... | collective-permute-start | bytes 589832 | tf_op jit(solution)/shard_map/ppermute | solution.py:19
  20.1 98.6 %collective-permute-start.4 = (bf16[1,512,192]{1,2,0:T(8,128)(2,1)}, bf16[1,512,192]{1,2,0:T(8,128)(2,1)}, u32[]{:S(2)}, u32[]{:S(2)}) collective-permute-start(bf16[1,512,192]{1,2,0:T(8,128)(2,1)} %get-tuple-element.139), channel_id=1, source_target_pairs={{0,12},{4,0},{8,4},{12,8},{1,13},{5,1},{9,5},{13,9},{2,14},{6,2},{... | collective-permute-start | bytes 589832 | tf_op jit(solution)/shard_map/ppermute | solution.py:22
  23.3 94.2 %collective-permute-start.6 = (bf16[1,512,192]{1,2,0:T(8,128)(2,1)}, bf16[1,512,192]{1,2,0:T(8,128)(2,1)}, u32[]{:S(2)}, u32[]{:S(2)}) collective-permute-start(bf16[1,512,192]{1,2,0:T(8,128)(2,1)} %get-tuple-element.131), channel_id=1, source_target_pairs={{0,4},{4,8},{8,12},{12,0},{1,5},{5,9},{9,13},{13,1},{2,6},{6,10},{... | collective-permute-start | bytes 589832 | tf_op jit(solution)/shard_map/ppermute | solution.py:19
  23.3 97.9 %collective-permute-start.7 = (bf16[1,512,192]{1,2,0:T(8,128)(2,1)}, bf16[1,512,192]{1,2,0:T(8,128)(2,1)}, u32[]{:S(2)}, u32[]{:S(2)}) collective-permute-start(bf16[1,512,192]{1,2,0:T(8,128)(2,1)} %get-tuple-element.131), channel_id=1, source_target_pairs={{0,12},{4,0},{8,4},{12,8},{1,13},{5,1},{9,5},{13,9},{2,14},{6,2},{... | collective-permute-start | bytes 589832 | tf_op jit(solution)/shard_map/ppermute | solution.py:22
  28.4 90.2 %collective-permute-start = (bf16[1,512,192]{1,2,0:T(8,128)(2,1)}, bf16[1,512,192]{1,2,0:T(8,128)(2,1)S(1)}, u32[]{:S(2)}, u32[]{:S(2)}) collective-permute-start(bf16[1,512,192]{1,2,0:T(8,128)(2,1)} %get-tuple-element.147), channel_id=1, source_target_pairs={{0,4},{4,8},{8,12},{12,0},{1,5},{5,9},{9,13},{13,1},{2,6},{6,10},{... | collective-permute-start | bytes 589832 | tf_op jit(solution)/shard_map/ppermute | solution.py:19
  103.6 426.6 %copy-start.172 = (f32[512]{0:T(512)}, f32[512]{0:T(512)S(1)}, u32[]{:S(2)}) copy-start(f32[512]{0:T(512)S(1)} %log_add_fusion.1) | copy-start | bytes 6148
  104.4 426.9 %copy-start.170 = (f32[512]{0:T(512)}, f32[512]{0:T(512)S(1)}, u32[]{:S(2)}) copy-start(f32[512]{0:T(512)S(1)} %log_add_fusion.2) | copy-start | bytes 6148
  115.5 6.8 collective-permute-start.1
  117.5 16.6 %collective-permute-start.5 = (bf16[1,512,192]{1,2,0:T(8,128)(2,1)S(1)}, bf16[1,512,192]{1,2,0:T(8,128)(2,1)S(1)}, u32[]{:S(2)}, u32[]{:S(2)}) collective-permute-start(bf16[1,512,192]{1,2,0:T(8,128)(2,1)S(1)} %collective-permute-done.3), channel_id=1, source_target_pairs={{0,4},{4,8},{8,12},{12,0},{1,5},{5,9},{9,13},{13,1},{2,6},{6,10},{... | collective-permute-start | bytes 589832 | tf_op jit(solution)/shard_map/ppermute | solution.py:19
  118.5 8.6 collective-permute-start.8
  118.6 22.3 %collective-permute-start.2 = (bf16[1,512,192]{1,2,0:T(8,128)(2,1)S(1)}, bf16[1,512,192]{1,2,0:T(8,128)(2,1)S(1)}, u32[]{:S(2)}, u32[]{:S(2)}) collective-permute-start(bf16[1,512,192]{1,2,0:T(8,128)(2,1)S(1)} %collective-permute-done), channel_id=1, source_target_pairs={{0,4},{4,8},{8,12},{12,0},{1,5},{5,9},{9,13},{13,1},{2,6},{6,10},{... | collective-permute-start | bytes 589832 | tf_op jit(solution)/shard_map/ppermute | solution.py:19
  152.7 98.9 %all-gather.6.cloned.1.call-start = ((), (), s32[]{:S(2)}) async-start(), calls=%async_computation.12 | async-start | bytes 1769472 | tf_op jit(solution)/shard_map/all_gather | solution.py:168
  153.3 110.9 %all-gather.8.cloned.1.call-start = ((), (), s32[]{:S(2)}) async-start(), calls=%async_computation.13 | async-start | bytes 1769472 | tf_op jit(solution)/shard_map/all_gather | solution.py:169
  153.9 218.9 %all-reduce.16.cloned.1.call-start = ((), (), s32[]{:S(2)}) async-start(), calls=%async_computation.28 | async-start | bytes 9437184 | tf_op jit(solution)/shard_map/psum | solution.py:202
  250.4 261.6 %copy-start.168 = (f32[512]{0:T(512)}, f32[512]{0:T(512)S(1)}, u32[]{:S(2)}) copy-start(f32[512]{0:T(512)S(1)} %broadcast_multiply_fusion.15) | copy-start | bytes 6148
  251.6 260.5 %copy-start.177 = (f32[512]{0:T(512)}, f32[512]{0:T(512)S(1)}, u32[]{:S(2)}) copy-start(f32[512]{0:T(512)S(1)} %add_rsqrt_fusion.3) | copy-start | bytes 6148
  278.1 217.3 %all-reduce.14.cloned.1.call-start = ((), (), s32[]{:S(2)}) async-start(), calls=%async_computation.27 | async-start | bytes 9437184 | tf_op jit(solution)/shard_map/psum | solution.py:226
  400.6 247.0 %reduce-scatter.25.cloned.1.call-start = ((), (), s32[]{:S(2)}) async-start(), calls=%async_computation.15 | async-start | bytes 1966080 | tf_op jit(solution)/shard_map/reduce_scatter | solution.py:247
  512.0 137.3 %reduce-scatter.29.cloned.1.call-start = ((), (), s32[]{:S(2)}) async-start(), calls=%async_computation.17 | async-start | bytes 1966080 | tf_op jit(solution)/shard_map/reduce_scatter | solution.py:247
  524.6 126.3 %reduce-scatter.33.cloned.1.call-start = ((), (), s32[]{:S(2)}) async-start(), calls=%async_computation.19 | async-start | bytes 1966080 | tf_op jit(solution)/shard_map/reduce_scatter | solution.py:247
  544.3 112.8 %reduce-scatter.23.cloned.1.call-start = ((), (), s32[]{:S(2)}) async-start(), calls=%async_computation.14 | async-start | bytes 1966080 | tf_op jit(solution)/shard_map/reduce_scatter | solution.py:246
  571.1 122.4 %reduce-scatter.27.cloned.1.call-start = ((), (), s32[]{:S(2)}) async-start(), calls=%async_computation.16 | async-start | bytes 1966080 | tf_op jit(solution)/shard_map/reduce_scatter | solution.py:246
  594.4 135.5 %reduce-scatter.31.cloned.1.call-start = ((), (), s32[]{:S(2)}) async-start(), calls=%async_computation.18 | async-start | bytes 1966080 | tf_op jit(solution)/shard_map/reduce_scatter | solution.py:246
  609.3 143.8 %reduce-scatter.45.cloned.1.call-start = ((), (), s32[]{:S(2)}) async-start(), calls=%async_computation.25 | async-start | bytes 1769472
  621.7 146.9 %reduce-scatter.43.cloned.1.call-start = ((), (), s32[]{:S(2)}) async-start(), calls=%async_computation.24 | async-start | bytes 589824
  641.0 142.8 %reduce-scatter.37.cloned.1.call-start = ((), (), s32[]{:S(2)}) async-start(), calls=%async_computation.21 | async-start | bytes 589824
  647.6 151.7 %reduce-scatter.41.cloned.1.call-start = ((), (), s32[]{:S(2)}) async-start(), calls=%async_computation.23 | async-start | bytes 589824
  653.4 161.0 %reduce-scatter.39.cloned.1.call-start = ((), (), s32[]{:S(2)}) async-start(), calls=%async_computation.22 | async-start | bytes 589824
  732.6 106.5 %reduce-scatter.35.cloned.1.call-start = ((), (), s32[]{:S(2)}) async-start(), calls=%async_computation.20 | async-start | bytes 1769472 | tf_op jit(solution)/shard_map/reduce_scatter | solution.py:286
  737.2 141.0 %all-reduce.12.cloned.1.call-start = ((), (), s32[]{:S(2)}) async-start(), calls=%async_computation.26 | async-start | bytes 9437184 | tf_op jit(solution)/shard_map/psum | solution.py:270
  747.1 176.0 %all-reduce.20.cloned.1.call-start = ((), (), s32[]{:S(2)}) async-start(), calls=%async_computation.30 | async-start | bytes 3538944 | tf_op jit(solution)/shard_map/psum | solution.py:294
  (215 other events, 1692.7 us)
Sparse Core Ops, SparseCore 0:
  152.8 93.7 all-reduce.17
  278.2 94.5 all-reduce.15
  400.8 94.5 all-reduce.13
  747.2 93.3 all-reduce.11
  844.4 78.6 all-reduce.19
Sparse Core Ops, SparseCore 1:
  154.7 22.0 all-gather.5
  178.2 22.6 all-gather.7
  512.0 35.4 reduce-scatter.24
  549.8 34.2 reduce-scatter.28
  586.4 34.1 reduce-scatter.32
  622.9 34.1 reduce-scatter.22
  659.3 34.1 reduce-scatter.26
  695.7 34.1 reduce-scatter.30
  732.6 20.5 reduce-scatter.44
  755.5 13.0 reduce-scatter.42
  770.7 13.0 reduce-scatter.36
  786.2 13.0 reduce-scatter.40
  801.3 13.0 reduce-scatter.38
  817.4 21.7 reduce-scatter.34
